TPU v7x, 32 devices: a whole 2x2x4 slice. The times are simulated.
32 devices in a mesh: section: 4 (over y, x), tp: 8 (over z, core).
Axes of the slice: x: 2, y: 2, z: 4, core: 2. Of those that a mesh axis runs over, the one named last changes fastest.
Arguments:
- inputs_now: bfloat16 [1536, 6144], P(('section', 'tp')), may hold values from -6 to 6
- cotangents: bfloat16 [1536, 6144], P(('section', 'tp')), may hold values from -6 to 6
- stashed: bfloat16 [3, 1536, 6144], P(None, ('section', 'tp')), may hold values from -6 to 6
- plan: int32 [4], replicated, may hold values from 0 to 2
- fwd_scores: bfloat16 [4, 48, 384, 384], P('section', 'tp'), may hold values from -9 to 300, as said below
- back_scores: bfloat16 [4, 48, 384, 384], P('section', 'tp'), may hold values from -9 to 300, as said below
- value_weight: bfloat16 [4, 6144, 6144], P('section', None, 'tp'), may hold values from -0.078125 to 0.078125
- out_weight: bfloat16 [4, 6144, 6144], P('section', 'tp'), may hold values from -0.21875 to 0.21875
Outputs:
- handed_on: bfloat16 [1536, 6144], P(('section', 'tp'))
- grad_back: bfloat16 [1536, 6144], P(('section', 'tp'))
- stash_next: bfloat16 [3, 1536, 6144], P(None, ('section', 'tp'))
- value_grad: bfloat16 [4, 6144, 6144], P('section', None, 'tp')
- out_grad: bfloat16 [4, 6144, 6144], P('section', 'tp')
Inputs may be any that keep to these rules, and one draw needn't show every extreme that they name: plan[s] names the slot, in the stash rows of section 3 - s, that holds section s's micro-batch for this tick's backward. `fwd_scores`: logits of keys later than the query are never read. `back_scores`: logits of keys later than the query are never read.
All inputs are finite; a program needn't handle non-finite values.
Results may differ from a plain program's by a relative error of at most 0.012.
Values may be sent and summed in bfloat16 or wider, within the bound.
A program may use at most 192 MiB of HBM per device.

v0:
```python
import jax
import jax.numpy as jnp
from jax import lax
from jax.sharding import PartitionSpec as P

HEAD = 128
eps = 1e-05


def passed_along(array, axis, by):
    size = lax.axis_size(axis)
    return lax.ppermute(array, axis, [(i, (i + by) % size) for i in range(size)])


def partner(value, axis, stride):
    mask = 2**stride
    pairs = [(source, source ^ mask) for source in range(lax.axis_size(axis))]
    return lax.ppermute(value, axis, pairs)


def normalize(layer_rows):
    average = jnp.mean(layer_rows, axis=-1, keepdims=True)
    centred = layer_rows - average
    inv_scale = lax.rsqrt(jnp.mean(centred * centred, axis=-1, keepdims=True) + eps)
    return (centred * inv_scale, inv_scale)


def causal_softmax(scores):
    logits = scores.astype(jnp.float32)
    rows = logits.shape[-1]
    causal = lax.broadcasted_iota(jnp.int32, (rows, rows), 0) >= lax.broadcasted_iota(
        jnp.int32, (rows, rows), 1
    )
    logits = jnp.where(causal, logits, -1e30)
    row_top = jnp.max(logits, axis=-1, keepdims=True)
    raised = jnp.where(causal, jnp.exp(logits - row_top), 0.0)
    return (raised / jnp.sum(raised, axis=-1, keepdims=True)).astype(jnp.bfloat16)


def mix_heads(weights, value_rows):
    rows = value_rows.shape[0]
    head_count = weights.shape[0]
    by_head = value_rows.reshape(rows, head_count, HEAD)
    mixed = jnp.einsum("hqk,khe->qhe", weights, by_head, preferred_element_type=jnp.float32)
    return mixed.reshape(rows, head_count * HEAD).astype(jnp.bfloat16)


def per_device(
    inputs_now, cotangents, stashed, plan, fwd_scores, back_scores, value_weight, out_weight
):
    tp_count = lax.axis_size("tp")
    sections = lax.axis_size("section")
    tp_index = lax.axis_index("tp")
    section_idx = lax.axis_index("section")
    mirror = sections - 1 - section_idx
    share_rows = inputs_now.shape[0]
    all_rows = share_rows * tp_count
    weight_in = value_weight[0]
    weight_out = out_weight[0]
    col_share = weight_in.shape[1]
    layer_rows = inputs_now.astype(jnp.float32)
    unit_rows, _ = normalize(layer_rows)
    normed = unit_rows.astype(jnp.bfloat16)
    values = jnp.dot(
        lax.all_gather(normed, "tp", axis=0, tiled=True),
        weight_in,
        preferred_element_type=jnp.float32,
    ).astype(jnp.bfloat16)
    context = mix_heads(causal_softmax(fwd_scores[0]), values)
    summed = lax.psum(
        jnp.dot(context, weight_out, preferred_element_type=jnp.float32).astype(jnp.bfloat16), "tp"
    ).astype(jnp.float32)
    branch = lax.dynamic_slice_in_dim(summed, tp_index * share_rows, share_rows, 0)
    layer_out = (layer_rows + branch).astype(jnp.bfloat16)
    handed_on = passed_along(layer_out, "section", 1)
    lookup = jnp.arange(sections, dtype=jnp.int32)
    owner_slot = jnp.sum(jnp.where(lookup == mirror, plan, 0))
    guest_rows = lax.dynamic_index_in_dim(stashed, owner_slot, 0, keepdims=False)
    outgoing = jnp.stack([guest_rows, inputs_now])
    incoming = outgoing
    for flip_bit in range(sections.bit_length() - 1):
        incoming = partner(incoming, "section", flip_bit)
    stored = incoming[0]
    arrived = incoming[1]
    stash_next = lax.dynamic_update_index_in_dim(stashed, arrived, owner_slot, 0)
    stash_unit, stash_scale = normalize(stored.astype(jnp.float32))
    stash_normed = stash_unit.astype(jnp.bfloat16)
    piece_norm = lax.all_gather(stash_normed, "tp", axis=0, tiled=True)
    piece_cot = lax.all_gather(cotangents, "tp", axis=0, tiled=True)
    rows_norm = piece_norm
    rows_cot = piece_cot
    piece_value = jnp.dot(piece_norm, weight_in, preferred_element_type=jnp.float32).astype(
        jnp.bfloat16
    )
    rows_value = piece_value
    piece_grad = jnp.einsum(
        "td,hd->th", piece_cot, weight_out, preferred_element_type=jnp.float32
    ).astype(jnp.bfloat16)
    rows_grad = piece_grad
    rows_norm, rows_cot, rows_value, rows_grad = (rows_norm, rows_cot, rows_value, rows_grad)
    back_probs = causal_softmax(back_scores[0])
    stash_context = mix_heads(back_probs, rows_value)
    grad_outw = jnp.einsum("th,td->hd", stash_context, rows_cot, preferred_element_type=jnp.float32)
    head_count = back_probs.shape[0]
    value_back = (
        jnp.einsum(
            "hqk,qhe->khe",
            back_probs,
            rows_grad.reshape(all_rows, head_count, HEAD),
            preferred_element_type=jnp.float32,
        )
        .reshape(all_rows, col_share)
        .astype(jnp.bfloat16)
    )
    grad_valw = jnp.einsum("td,th->dh", rows_norm, value_back, preferred_element_type=jnp.float32)
    summed_back = lax.psum(
        jnp.einsum("th,dh->td", value_back, weight_in, preferred_element_type=jnp.float32).astype(
            jnp.bfloat16
        ),
        "tp",
    ).astype(jnp.float32)
    norm_grad = lax.dynamic_slice_in_dim(summed_back, tp_index * share_rows, share_rows, 0)
    input_grad = cotangents.astype(jnp.float32) + stash_scale * (
        norm_grad
        - jnp.mean(norm_grad, axis=-1, keepdims=True)
        - stash_unit * jnp.mean(norm_grad * stash_unit, axis=-1, keepdims=True)
    )
    grad_back = passed_along(input_grad.astype(jnp.bfloat16), "section", -1)
    return (
        handed_on,
        grad_back,
        stash_next,
        grad_valw.astype(jnp.bfloat16)[None],
        grad_outw.astype(jnp.bfloat16)[None],
    )


def solution(mesh):
    return jax.shard_map(
        per_device,
        mesh=mesh,
        in_specs=(
            P(("section", "tp"), None),
            P(("section", "tp"), None),
            P(None, ("section", "tp"), None),
            P(),
            P("section", "tp", None, None),
            P("section", "tp", None, None),
            P("section", None, "tp"),
            P("section", "tp", None),
        ),
        out_specs=(
            P(("section", "tp"), None),
            P(("section", "tp"), None),
            P(None, ("section", "tp"), None),
            P("section", None, "tp"),
            P("section", "tp", None),
        ),
        check_vma=False,
    )
```

profile of v0, /device:TPU:0, one launch (start us, length us, event | category | flops | bytes accessed | tf_op | source)
XLA Modules:
  0.0 429.3 jit_solution(4196626282191384859)
XLA Ops:
  7.2 2.9 copy.25
  10.1 0.2 convert_reduce_fusion.1
  10.3 0.3 fusion.47
  10.7 1.0 fusion.48
  11.8 0.7 all-gather.6.cloned.1.call-update
  12.6 5.9 %fusion.64 = (f32[6,384]{1,0:T(8,128)S(1)}, f32[6,384,384]{2,1,0:T(8,128)}) fusion(bf16[1,6,384,384]{3,2,1,0:T(8,128)(2,1)} %param.12, pred[384,384]{1,0:T(8,128)(4,1)S(1)} %iota_compare_fusion), kind=kOutput, calls=%fused_computation.81 | output fusion | flops 6193535 | bytes 5465088 | tf_op jit(solution)/shard_map/sub | solution.py:36
  18.5 2.2 fusion.65
  20.7 0.4 divide_convert_fusion
  21.1 44.7 %all-gather.4.cloned.1.call-done = bf16[384,6144]{1,0:T(8,128)(2,1)} async-done(((bf16[48,6144]{1,0:T(8,128)(2,1)}), bf16[384,6144]{1,0:T(8,128)(2,1)}) %all-gather.4.cloned.1.call-update) | async-done | bytes 4718608 | tf_op jit(solution)/shard_map/all_gather | solution.py:65
  65.8 8.9 %fusion.38 = bf16[384,768]{1,0:T(8,128)(2,1)S(1)} fusion(bf16[384,6144]{1,0:T(8,128)(2,1)} %all-gather.4.cloned.1.call-done, bf16[1,6144,768]{2,1,0:T(8,128)(2,1)} %param.14), kind=kOutput, calls=%fused_computation.48 | convolution fusion | flops 3624173568 | bytes 14745600 | tf_op jit(solution)/shard_map/dot_general | solution.py:64
  74.7 0.3 copy.16
  75.0 2.8 fusion.37
  77.8 9.5 %fusion.17 = bf16[384,6144]{1,0:T(8,128)(2,1)} fusion(bf16[384,768]{0,1:T(8,128)(2,1)S(1)} %bitcast.100, bf16[1,768,6144]{2,1,0:T(8,128)(2,1)} %param.15), kind=kOutput, calls=%fused_computation.17 | convolution fusion | flops 3626237952 | bytes 14745600 | tf_op jit(solution)/shard_map/dot_general | solution.py:71
  87.3 30.2 %all-gather.6.cloned.1.call-done = bf16[384,6144]{1,0:T(8,128)(2,1)} async-done(((bf16[48,6144]{1,0:T(8,128)(2,1)}), bf16[384,6144]{1,0:T(8,128)(2,1)}) %all-gather.6.cloned.1.call-update) | async-done | bytes 4718608 | tf_op jit(solution)/shard_map/all_gather | solution.py:89
  117.4 9.0 %fusion.44 = bf16[384,768]{1,0:T(8,128)(2,1)S(1)} fusion(bf16[384,6144]{1,0:T(8,128)(2,1)} %all-gather.6.cloned.1.call-done, bf16[1,768,6144]{2,1,0:T(8,128)(2,1)} %param.15), kind=kOutput, calls=%fused_computation.50 | convolution fusion | flops 3624173568 | bytes 14745600 | tf_op jit(solution)/shard_map/td,hd->th/dot_general | solution.py:96
  126.4 0.3 copy.17
  126.7 0.5 convolution_convert_fusion.3
  127.3 0.8 copy-done.3
  128.1 14.5 %fusion.14 = bf16[384,6144]{1,0:T(8,128)(2,1)} fusion(bf16[384,768]{0,1:T(8,128)(2,1)S(1)} %bitcast.102, bf16[1,6144,768]{2,1,0:T(8,128)(2,1)} %param.14), kind=kOutput, calls=%fused_computation.16 | convolution fusion | flops 3626237952 | bytes 14745600 | tf_op jit(solution)/shard_map/th,dh->td/dot_general | solution.py:117
  142.6 0.0 all-gather.8.cloned.1.call-start
  142.7 0.6 copy-done.6
  143.3 0.6 fusion.61
  145.8 1.2 constant_dynamic-slice_fusion
  147.0 0.1 pad_maximum_fusion
  147.1 1.4 collective-permute-start.1
  148.6 26.8 %collective-permute-done.1 = bf16[2,48,6144]{2,1,0:T(8,128)(2,1)} collective-permute-done((bf16[2,48,6144]{2,1,0:T(8,128)(2,1)S(1)}, bf16[2,48,6144]{2,1,0:T(8,128)(2,1)}, u32[]{:S(2)}, u32[]{:S(2)}) %collective-permute-start.1) | collective-permute-done | bytes 1179680 | tf_op jit(solution)/shard_map/ppermute | solution.py:18
  175.4 1.4 collective-permute-start.2
  176.8 26.0 %collective-permute-done.2 = bf16[2,48,6144]{2,1,0:T(8,128)(2,1)S(1)} collective-permute-done((bf16[2,48,6144]{2,1,0:T(8,128)(2,1)}, bf16[2,48,6144]{2,1,0:T(8,128)(2,1)S(1)}, u32[]{:S(2)}, u32[]{:S(2)}) %collective-permute-start.2) | collective-permute-done | bytes 1179680 | tf_op jit(solution)/shard_map/ppermute | solution.py:18
  202.8 0.2 convert_reduce_fusion.2
  203.0 0.3 fusion.58
  203.4 133.5 %all-reduce.3.cloned.1.call-done = (bf16[384,6144]{1,0:T(8,128)(2,1)}, bf16[384,6144]{1,0:T(8,128)(2,1)}) async-done(((bf16[384,6144]{1,0:T(8,128)(2,1)}, bf16[384,6144]{1,0:T(8,128)(2,1)}), (bf16[384,6144]{1,0:T(8,128)(2,1)}, bf16[384,6144]{1,0:T(8,128)(2,1)})) %all-reduce.3.cloned.1.call-update) | async-done | bytes 9437200 | tf_op jit(solution)/shard_map/psum | solution.py:70
  336.9 1.5 convert_reduce_fusion
  338.4 2.7 fusion.52
  341.1 1.2 fusion.59
  342.3 1.5 collective-permute-start
  343.9 1.5 collective-permute-start.3
  345.3 0.9 slice_dynamic-update-slice_fusion
  346.2 13.3 %collective-permute-done = bf16[48,6144]{1,0:T(8,128)(2,1)S(1)} collective-permute-done((bf16[48,6144]{1,0:T(8,128)(2,1)S(1)}, bf16[48,6144]{1,0:T(8,128)(2,1)S(1)}, u32[]{:S(2)}, u32[]{:S(2)}) %collective-permute-start) | collective-permute-done | bytes 589856 | tf_op jit(solution)/shard_map/ppermute | solution.py:12
  359.5 11.3 %collective-permute-done.3 = bf16[48,6144]{1,0:T(8,128)(2,1)} collective-permute-done((bf16[48,6144]{1,0:T(8,128)(2,1)}, bf16[48,6144]{1,0:T(8,128)(2,1)}, u32[]{:S(2)}, u32[]{:S(2)}) %collective-permute-start.3) | collective-permute-done | bytes 589856 | tf_op jit(solution)/shard_map/ppermute | solution.py:12
  370.8 21.8 %all-gather.8.cloned.1.call-done = bf16[384,6144]{1,0:T(8,128)(2,1)} async-done(((bf16[48,6144]{1,0:T(8,128)(2,1)}), bf16[384,6144]{1,0:T(8,128)(2,1)}) %all-gather.8.cloned.1.call-update) | async-done | bytes 4718608 | tf_op jit(solution)/shard_map/all_gather | solution.py:88
  392.6 8.9 %fusion.41 = bf16[384,768]{1,0:T(8,128)(2,1)S(1)} fusion(bf16[384,6144]{1,0:T(8,128)(2,1)} %all-gather.8.cloned.1.call-done, bf16[1,6144,768]{2,1,0:T(8,128)(2,1)} %param.14), kind=kOutput, calls=%fused_computation.49 | convolution fusion | flops 3624173568 | bytes 14745600 | tf_op jit(solution)/shard_map/dot_general | solution.py:92
  401.6 0.3 copy.18
  401.9 0.7 convolution_convert_fusion.2
  402.6 0.1 copy-done.4
  402.6 9.9 %fusion.12 = bf16[1,6144,768]{2,1,0:T(8,128)(2,1)} fusion(bf16[384,6144]{1,0:T(8,128)(2,1)} %all-gather.8.cloned.1.call-done, bf16[384,768]{0,1:T(8,128)(2,1)S(1)} %bitcast.103), kind=kOutput, calls=%fused_computation.14 | convolution fusion | flops 3628597248 | bytes 14745600 | tf_op jit(solution)/shard_map/td,th->dh/dot_general | solution.py:115
  412.5 7.4 %fusion.13 = bf16[1,768,6144]{2,1,0:T(8,128)(2,1)} fusion(bf16[384,768]{0,1:T(8,128)(2,1)S(1)} %bitcast.104, bf16[384,6144]{1,0:T(8,128)(2,1)S(1)} %bitcast.106), kind=kOutput, calls=%fused_computation.15 | convolution fusion | flops 3628597248 | bytes 14745600 | tf_op jit(solution)/shard_map/th,td->hd/dot_general | solution.py:103
  420.0 0.8 copy.26
  420.8 1.9 copy.27
  (28 shorter events, 0.3 us)
Async XLA Ops:
  7.2 2.9 copy-start
  7.2 58.6 %all-gather.4.cloned.1.call-start = ((), (), s32[]{:S(2)}) async-start(), calls=%async_computation | async-start | bytes 5308416 | tf_op jit(solution)/shard_map/all_gather | solution.py:65
  11.7 105.7 %all-gather.6.cloned.1.call-start = ((), (), s32[]{:S(2)}) async-start(), calls=%async_computation.1 | async-start | bytes 5308416 | tf_op jit(solution)/shard_map/all_gather | solution.py:89
  12.5 324.4 %all-reduce.3.cloned.1.call-start = ((), (), s32[]{:S(2)}) async-start(), calls=%async_computation.3 | async-start | bytes 18874368 | tf_op jit(solution)/shard_map/psum | solution.py:70
  12.6 5.9 %copy-start.5 = (bf16[1,6,384,384]{3,2,1,0:T(8,128)(2,1)S(1)}, bf16[1,6,384,384]{3,2,1,0:T(8,128)(2,1)}, u32[]{:S(2)}) copy-start(bf16[1,6,384,384]{3,2,1,0:T(8,128)(2,1)} %param.13) | copy-start | bytes 5308420
  127.3 0.8 copy-start.3
  142.6 0.7 copy-start.6
  142.6 250.0 %all-gather.8.cloned.1.call-start = ((), (), s32[]{:S(2)}) async-start(), calls=%async_computation.2 | async-start | bytes 5308416 | tf_op jit(solution)/shard_map/all_gather | solution.py:88
  147.1 28.2 %collective-permute-start.1 = (bf16[2,48,6144]{2,1,0:T(8,128)(2,1)S(1)}, bf16[2,48,6144]{2,1,0:T(8,128)(2,1)}, u32[]{:S(2)}, u32[]{:S(2)}) collective-permute-start(bf16[2,48,6144]{2,1,0:T(8,128)(2,1)S(1)} %pad_maximum_fusion), channel_id=1, source_target_pairs={{0,8},{8,0},{16,24},{24,16},{1,9},{9,1},{17,25},{25,17},{2,10},{10... | collective-permute-start | bytes 3538952 | tf_op jit(solution)/shard_map/ppermute | solution.py:18
  175.4 27.4 %collective-permute-start.2 = (bf16[2,48,6144]{2,1,0:T(8,128)(2,1)}, bf16[2,48,6144]{2,1,0:T(8,128)(2,1)S(1)}, u32[]{:S(2)}, u32[]{:S(2)}) collective-permute-start(bf16[2,48,6144]{2,1,0:T(8,128)(2,1)} %collective-permute-done.1), channel_id=1, source_target_pairs={{0,16},{8,24},{16,0},{24,8},{1,17},{9,25},{17,1},{25,9},{2,18},{10... | collective-permute-start | bytes 3538952 | tf_op jit(solution)/shard_map/ppermute | solution.py:18
  342.3 17.2 %collective-permute-start = (bf16[48,6144]{1,0:T(8,128)(2,1)S(1)}, bf16[48,6144]{1,0:T(8,128)(2,1)S(1)}, u32[]{:S(2)}, u32[]{:S(2)}) collective-permute-start(bf16[48,6144]{1,0:T(8,128)(2,1)S(1)} %fusion.59), channel_id=1, source_target_pairs={{0,8},{8,16},{16,24},{24,0},{1,9},{9,17},{17,25},{25,1},{2,10},{10... | collective-permute-start | bytes 1769480 | tf_op jit(solution)/shard_map/ppermute | solution.py:12
  343.9 26.9 %collective-permute-start.3 = (bf16[48,6144]{1,0:T(8,128)(2,1)}, bf16[48,6144]{1,0:T(8,128)(2,1)}, u32[]{:S(2)}, u32[]{:S(2)}) collective-permute-start(bf16[48,6144]{1,0:T(8,128)(2,1)} %get-tuple-element.10), channel_id=1, source_target_pairs={{0,24},{8,0},{16,8},{24,16},{1,25},{9,1},{17,9},{25,17},{2,26},{10... | collective-permute-start | bytes 1769480 | tf_op jit(solution)/shard_map/ppermute | solution.py:12
  359.5 33.1 %copy-start.1 = (bf16[48,6144]{1,0:T(8,128)(2,1)}, bf16[48,6144]{1,0:T(8,128)(2,1)S(1)}, u32[]{:S(2)}) copy-start(bf16[48,6144]{1,0:T(8,128)(2,1)S(1)} %collective-permute-done) | copy-start | bytes 1769476
  401.6 1.1 copy-start.4
  401.9 10.7 %slice-start = ((s8[4718592]{0:T(1024)(128)(4,1)}), s8[4194304]{0:T(1024)(128)(4,1)S(1)}, s32[]{:S(2)}) async-start(s8[4718592]{0:T(1024)(128)(4,1)} %bitcast.105), calls=%async_computation.4 | async-start | bytes 8388608
  402.6 9.9 %slice-start.1 = ((s8[4718592]{0:T(1024)(128)(4,1)}), s8[524288]{0:T(1024)(128)(4,1)S(1)}, s32[]{:S(2)}) async-start(s8[4718592]{0:T(1024)(128)(4,1)} %bitcast.105), calls=%async_computation.5 | async-start | bytes 1048576
  412.5 7.5 %copy-start.2 = (bf16[48,6144]{1,0:T(8,128)(2,1)S(1)}, bf16[48,6144]{1,0:T(8,128)(2,1)}, u32[]{:S(2)}) copy-start(bf16[48,6144]{1,0:T(8,128)(2,1)} %copy-done.1) | copy-start | bytes 1769476
Sparse Core Ops, SparseCore 0:
  11.8 53.9 all-gather.3
  67.4 49.9 all-gather.5
  142.7 194.0 all-reduce.2
  341.3 51.3 all-gather.7
where the time goes:
time: 430 us; the launch traced here: 429 us
  waiting for transfers between devices  308 us (72%)
  matrix products  72.1 us (17%)
  other arithmetic  16.9 us (4%)
  between operations  15.9 us (4%)
  local copies, waits for them, and re-layouts  10.1 us (2%)
  starting transfers between devices  5.99 us (1%)
    psum x1, waiting for transfers between devices, per_device(): lax.psum(jnp.dot(context, weight_out, preferred_element_type=jnp.float32)...  134 us
    ppermute x2, waiting for transfers between devices, partner(): return lax.ppermute(value, axis, pairs)  52.8 us
    all_gather x1, waiting for transfers between devices, per_device(): lax.all_gather(normed, 'tp', axis=0, tiled=True)  44.7 us
    all_gather x1, waiting for transfers between devices, per_device(): piece_cot = lax.all_gather(cotangents, 'tp', axis=0, tiled=True)  30.2 us
    ppermute x2, waiting for transfers between devices, passed_along(): lax.ppermute(array, axis, [(i, (i + by) % size) for i in range(size)])  24.6 us
    all_gather x1, waiting for transfers between devices, per_device(): piece_norm = lax.all_gather(stash_normed, 'tp', axis=0, tiled=True)  21.8 us
    dot_general x1, matrix products, per_device(): jnp.einsum('th,dh->td', value_back, weight_in, preferred_element_type=jnp...  14.5 us
    dot_general x1, matrix products, per_device(): jnp.einsum('td,th->dh', rows_norm, value_back, preferred_element_type=jnp...  9.91 us
  transfers between devices with their start and end apart: 8, of which 8 were waited for; matrix products, arithmetic and copies ran while one was open for 8% of the time, Pallas kernels for 0%

commit v1 on v0

--- a/solution.py
+++ b/solution.py
@@ -5,6 +5,12 @@
 
 HEAD = 128
 eps = 1e-05
+
+
+def add_all(x, name):
+    terms = lax.all_gather(x, name, axis=0, tiled=False)
+    total = terms.sum(axis=0)
+    return total
 
 
 def passed_along(array, axis, by):
@@ -67,7 +73,7 @@
         preferred_element_type=jnp.float32,
     ).astype(jnp.bfloat16)
     context = mix_heads(causal_softmax(fwd_scores[0]), values)
-    summed = lax.psum(
+    summed = add_all(
         jnp.dot(context, weight_out, preferred_element_type=jnp.float32).astype(jnp.bfloat16), "tp"
     ).astype(jnp.float32)
     branch = lax.dynamic_slice_in_dim(summed, tp_index * share_rows, share_rows, 0)

time: 430 us -> 668 us (1.55)
  waiting for transfers between devices: 308 us -> 524 us
  other arithmetic: 16.9 us -> 32.5 us
    all_gather x0 -> x1, waiting for transfers between devices: none -> 304 us  [add_all(): terms = lax.all_gather(x, name, axis=0, tiled=False)]
    psum x1, waiting for transfers between devices: 134 us -> 42.5 us  [per_device(): lax.psum(jnp.einsum('th,dh->td', value_back, weight_in, preferred_element...]
    all_gather x1, waiting for transfers between devices: 30.2 us -> 51.4 us  [per_device(): piece_cot = lax.all_gather(cotangents, 'tp', axis=0, tiled=True)]
    reduce_sum x0 -> x1, other arithmetic: none -> 15.8 us  [add_all(): total = terms.sum(axis=0)]
    all_gather x1, waiting for transfers between devices: 21.8 us -> 11.8 us  [per_device(): piece_norm = lax.all_gather(stash_normed, 'tp', axis=0, tiled=True)]
    ppermute x2, waiting for transfers between devices: 24.6 us -> 17.7 us  [passed_along(): lax.ppermute(array, axis, [(i, (i + by) % size) for i in range(size)])]
  transfers between devices with their start and end apart: 8 -> 9, of which waited for: 8 -> 9; matrix products, arithmetic and copies ran while one was open for 8% -> 11% of each run, Pallas kernels for 0% -> 0%
where the time goes in v1:
time: 668 us
  waiting for transfers between devices  524 us (78%)
  matrix products  76.6 us (11%)
  other arithmetic  32.5 us (5%)
  between operations  15.9 us (2%)
  local copies, waits for them, and re-layouts  11.4 us (2%)
  starting transfers between devices  7.65 us (1%)
    all_gather x1, waiting for transfers between devices, add_all(): terms = lax.all_gather(x, name, axis=0, tiled=False)  304 us
    ppermute x2, waiting for transfers between devices, partner(): return lax.ppermute(value, axis, pairs)  52.7 us
    all_gather x1, waiting for transfers between devices, per_device(): piece_cot = lax.all_gather(cotangents, 'tp', axis=0, tiled=True)  51.4 us
    all_gather x1, waiting for transfers between devices, per_device(): lax.all_gather(normed, 'tp', axis=0, tiled=True)  43.1 us
    psum x1, waiting for transfers between devices, per_device(): lax.psum(jnp.einsum('th,dh->td', value_back, weight_in, preferred_element...  42.5 us
    ppermute x2, waiting for transfers between devices, passed_along(): lax.ppermute(array, axis, [(i, (i + by) % size) for i in range(size)])  17.7 us
    reduce_sum x1, other arithmetic, add_all(): total = terms.sum(axis=0)  15.8 us
    dot_general x1, matrix products, per_device(): jnp.einsum('th,dh->td', value_back, weight_in, preferred_element_type=jnp...  14.7 us
  transfers between devices with their start and end apart: 9, of which 9 were waited for; matrix products, arithmetic and copies ran while one was open for 11% of the time, Pallas kernels for 0%

profile of v1, /device:TPU:0, one launch (start us, length us, event | category | flops | bytes accessed | tf_op | source)
XLA Modules:
  0.0 667.8 jit_solution(3428280623607217348)
XLA Ops:
  7.2 3.0 copy.24
  10.2 0.0 all-reduce.2.cloned.1.call-start
  10.3 2.1 fusion.65
  12.5 0.4 divide_convert_fusion
  12.8 51.4 %all-gather.8.cloned.1.call-done = bf16[384,6144]{1,0:T(8,128)(2,1)} async-done(((bf16[48,6144]{1,0:T(8,128)(2,1)}), bf16[384,6144]{1,0:T(8,128)(2,1)}) %all-gather.8.cloned.1.call-update) | async-done | bytes 4718608 | tf_op jit(solution)/shard_map/all_gather | solution.py:95
  64.3 9.0 %fusion.44 = bf16[384,768]{1,0:T(8,128)(2,1)S(1)} fusion(bf16[384,6144]{1,0:T(8,128)(2,1)} %all-gather.8.cloned.1.call-done, bf16[1,768,6144]{2,1,0:T(8,128)(2,1)} %param.15), kind=kOutput, calls=%fused_computation.50 | convolution fusion | flops 3624173568 | bytes 14745600 | tf_op jit(solution)/shard_map/td,hd->th/dot_general | solution.py:102
  73.3 0.3 copy.17
  73.6 0.5 convolution_convert_fusion.3
  74.1 14.7 %fusion.14 = bf16[384,6144]{1,0:T(8,128)(2,1)} fusion(bf16[384,768]{0,1:T(8,128)(2,1)S(1)} %bitcast.104, bf16[1,6144,768]{2,1,0:T(8,128)(2,1)} %param.14), kind=kOutput, calls=%fused_computation.16 | convolution fusion | flops 3626237952 | bytes 14745600 | tf_op jit(solution)/shard_map/th,dh->td/dot_general | solution.py:123
  88.9 1.0 copy-done
  89.9 0.2 convert_reduce_fusion.1
  90.1 0.3 fusion.47
  90.5 1.0 fusion.48
  91.6 0.6 fusion.61
  94.2 1.1 constant_dynamic-slice_fusion
  95.3 0.1 pad_maximum_fusion
  95.4 1.5 collective-permute-start.1
  96.9 26.7 %collective-permute-done.1 = bf16[2,48,6144]{2,1,0:T(8,128)(2,1)} collective-permute-done((bf16[2,48,6144]{2,1,0:T(8,128)(2,1)S(1)}, bf16[2,48,6144]{2,1,0:T(8,128)(2,1)}, u32[]{:S(2)}, u32[]{:S(2)}) %collective-permute-start.1) | collective-permute-done | bytes 1179680 | tf_op jit(solution)/shard_map/ppermute | solution.py:24
  123.7 1.5 collective-permute-start.2
  125.1 26.0 %collective-permute-done.2 = bf16[2,48,6144]{2,1,0:T(8,128)(2,1)S(1)} collective-permute-done((bf16[2,48,6144]{2,1,0:T(8,128)(2,1)}, bf16[2,48,6144]{2,1,0:T(8,128)(2,1)S(1)}, u32[]{:S(2)}, u32[]{:S(2)}) %collective-permute-start.2) | collective-permute-done | bytes 1179680 | tf_op jit(solution)/shard_map/ppermute | solution.py:24
  151.1 0.2 convert_reduce_fusion.2
  151.3 0.3 fusion.58
  151.7 42.5 %all-reduce.2.cloned.1.call-done = bf16[384,6144]{1,0:T(8,128)(2,1)} async-done(((bf16[384,6144]{1,0:T(8,128)(2,1)}), bf16[384,6144]{1,0:T(8,128)(2,1)}) %all-reduce.2.cloned.1.call-update) | async-done | bytes 4718608 | tf_op jit(solution)/shard_map/psum | solution.py:122
  194.1 1.5 convert_reduce_fusion
  195.6 2.8 fusion.52
  198.4 0.2 all-gather.12.cloned.1.call-start
  198.7 5.9 fusion.64
  204.5 43.1 %all-gather.6.cloned.1.call-done = bf16[384,6144]{1,0:T(8,128)(2,1)} async-done(((bf16[48,6144]{1,0:T(8,128)(2,1)}), bf16[384,6144]{1,0:T(8,128)(2,1)}) %all-gather.6.cloned.1.call-update) | async-done | bytes 4718608 | tf_op jit(solution)/shard_map/all_gather | solution.py:71
  247.7 9.7 %fusion.38 = bf16[384,768]{1,0:T(8,128)(2,1)} fusion(bf16[384,6144]{1,0:T(8,128)(2,1)} %all-gather.6.cloned.1.call-done, bf16[1,6144,768]{2,1,0:T(8,128)(2,1)} %param.14), kind=kOutput, calls=%fused_computation.48 | convolution fusion | flops 3624173568 | bytes 14745600 | tf_op jit(solution)/shard_map/dot_general | solution.py:70
  257.4 2.1 copy.16
  259.5 2.9 fusion.37
  262.5 9.3 %fusion.17 = bf16[384,6144]{1,0:T(8,128)(2,1)} fusion(bf16[384,768]{0,1:T(8,128)(2,1)S(1)} %bitcast.102, bf16[1,768,6144]{2,1,0:T(8,128)(2,1)} %param.15), kind=kOutput, calls=%fused_computation.17 | convolution fusion | flops 3626237952 | bytes 14745600 | tf_op jit(solution)/shard_map/dot_general | solution.py:77
  271.8 2.7 collective-permute-start.3
  274.5 0.9 slice_dynamic-update-slice_fusion
  275.4 12.5 %collective-permute-done.3 = bf16[48,6144]{1,0:T(8,128)(2,1)} collective-permute-done((bf16[48,6144]{1,0:T(8,128)(2,1)}, bf16[48,6144]{1,0:T(8,128)(2,1)}, u32[]{:S(2)}, u32[]{:S(2)}) %collective-permute-start.3) | collective-permute-done | bytes 589856 | tf_op jit(solution)/shard_map/ppermute | solution.py:18
  287.9 11.8 %all-gather.10.cloned.1.call-done = bf16[384,6144]{1,0:T(8,128)(2,1)} async-done(((bf16[48,6144]{1,0:T(8,128)(2,1)}), bf16[384,6144]{1,0:T(8,128)(2,1)}) %all-gather.10.cloned.1.call-update) | async-done | bytes 4718608 | tf_op jit(solution)/shard_map/all_gather | solution.py:94
  299.7 8.9 %fusion.41 = bf16[384,768]{1,0:T(8,128)(2,1)S(1)} fusion(bf16[384,6144]{1,0:T(8,128)(2,1)} %all-gather.10.cloned.1.call-done, bf16[1,6144,768]{2,1,0:T(8,128)(2,1)} %param.14), kind=kOutput, calls=%fused_computation.49 | convolution fusion | flops 3624173568 | bytes 14745600 | tf_op jit(solution)/shard_map/dot_general | solution.py:98
  308.7 0.3 copy.18
  309.0 0.7 convolution_convert_fusion.2
  309.7 11.0 %fusion.12 = bf16[1,6144,768]{2,1,0:T(8,128)(2,1)} fusion(bf16[384,6144]{1,0:T(8,128)(2,1)} %all-gather.10.cloned.1.call-done, bf16[384,768]{0,1:T(8,128)(2,1)} %bitcast.105), kind=kOutput, calls=%fused_computation.14 | convolution fusion | flops 3628597248 | bytes 14745600 | tf_op jit(solution)/shard_map/td,th->dh/dot_general | solution.py:121
  320.7 304.4 %all-gather.12.cloned.1.call-done = bf16[3072,6144]{1,0:T(8,128)(2,1)} async-done(((bf16[384,6144]{1,0:T(8,128)(2,1)}), bf16[3072,6144]{1,0:T(8,128)(2,1)}) %all-gather.12.cloned.1.call-update) | async-done | bytes 37748752 | tf_op jit(solution)/shard_map/all_gather | solution.py:11
  625.1 15.8 %reduce_sum.96 = bf16[384,6144]{1,0:T(8,128)(2,1)} reduce(bf16[8,384,6144]{2,1,0:T(8,128)(2,1)} %bitcast.98, bf16[]{:T(256)} %constant.35.clone.1), dimensions={0}, to_apply=%region_4.5 | reduce | flops 16515072 | bytes 42467328 | tf_op jit(solution)/shard_map/reduce_sum | solution.py:12
  640.9 1.2 fusion.59
  642.1 1.5 collective-permute-start
  643.6 9.8 %fusion.13 = bf16[1,768,6144]{2,1,0:T(8,128)(2,1)} fusion(bf16[384,768]{0,1:T(8,128)(2,1)S(1)} %bitcast.106, bf16[384,6144]{1,0:T(8,128)(2,1)} %all-gather.8.cloned.1.call-done), kind=kOutput, calls=%fused_computation.15 | convolution fusion | flops 3628597248 | bytes 14745600 | tf_op jit(solution)/shard_map/th,td->hd/dot_general | solution.py:109
  653.4 5.2 collective-permute-done
  658.5 0.8 copy.25
  659.4 1.9 copy.26
  (23 shorter events, 0.3 us)
Async XLA Ops:
  7.2 3.1 copy-start.3
  7.2 57.1 %all-gather.8.cloned.1.call-start = ((), (), s32[]{:S(2)}) async-start(), calls=%async_computation.1 | async-start | bytes 5308416 | tf_op jit(solution)/shard_map/all_gather | solution.py:95
  10.2 183.9 %all-reduce.2.cloned.1.call-start = ((), (), s32[]{:S(2)}) async-start(), calls=%async_computation.2 | async-start | bytes 9437184 | tf_op jit(solution)/shard_map/psum | solution.py:122
  10.3 2.1 copy-start.2
  74.1 14.7 %copy-start.1 = (bf16[6,128,384]{2,1,0:T(8,128)(2,1)}, bf16[6,128,384]{2,1,0:T(8,128)(2,1)S(1)}, u32[]{:S(2)}) copy-start(bf16[6,128,384]{2,1,0:T(8,128)(2,1)S(1)} %convolution_convert_fusion.3) | copy-start | bytes 1769476
  88.8 1.1 copy-start
  88.8 2.7 copy-start.4
  88.9 158.8 %all-gather.6.cloned.1.call-start = ((), (), s32[]{:S(2)}) async-start(), calls=%async_computation | async-start | bytes 5308416 | tf_op jit(solution)/shard_map/all_gather | solution.py:71
  91.5 208.2 %all-gather.10.cloned.1.call-start = ((), (), s32[]{:S(2)}) async-start(), calls=%async_computation.3 | async-start | bytes 5308416 | tf_op jit(solution)/shard_map/all_gather | solution.py:94
  95.4 28.3 %collective-permute-start.1 = (bf16[2,48,6144]{2,1,0:T(8,128)(2,1)S(1)}, bf16[2,48,6144]{2,1,0:T(8,128)(2,1)}, u32[]{:S(2)}, u32[]{:S(2)}) collective-permute-start(bf16[2,48,6144]{2,1,0:T(8,128)(2,1)S(1)} %pad_maximum_fusion), channel_id=1, source_target_pairs={{0,8},{8,0},{16,24},{24,16},{1,9},{9,1},{17,25},{25,17},{2,10},{10... | collective-permute-start | bytes 3538952 | tf_op jit(solution)/shard_map/ppermute | solution.py:24
  123.7 27.5 %collective-permute-start.2 = (bf16[2,48,6144]{2,1,0:T(8,128)(2,1)}, bf16[2,48,6144]{2,1,0:T(8,128)(2,1)S(1)}, u32[]{:S(2)}, u32[]{:S(2)}) collective-permute-start(bf16[2,48,6144]{2,1,0:T(8,128)(2,1)} %collective-permute-done.1), channel_id=1, source_target_pairs={{0,16},{8,24},{16,0},{24,8},{1,17},{9,25},{17,1},{25,9},{2,18},{10... | collective-permute-start | bytes 3538952 | tf_op jit(solution)/shard_map/ppermute | solution.py:24
  198.4 426.7 %all-gather.12.cloned.1.call-start = ((), (), s32[]{:S(2)}) async-start(), calls=%async_computation.4 | async-start | bytes 42467328 | tf_op jit(solution)/shard_map/all_gather | solution.py:11
  271.8 16.1 %collective-permute-start.3 = (bf16[48,6144]{1,0:T(8,128)(2,1)}, bf16[48,6144]{1,0:T(8,128)(2,1)}, u32[]{:S(2)}, u32[]{:S(2)}) collective-permute-start(bf16[48,6144]{1,0:T(8,128)(2,1)} %get-tuple-element.8), channel_id=1, source_target_pairs={{0,24},{8,0},{16,8},{24,16},{1,25},{9,1},{17,9},{25,17},{2,26},{10... | collective-permute-start | bytes 1769480 | tf_op jit(solution)/shard_map/ppermute | solution.py:18
  642.1 16.4 %collective-permute-start = (bf16[48,6144]{1,0:T(8,128)(2,1)S(1)}, bf16[48,6144]{1,0:T(8,128)(2,1)S(1)}, u32[]{:S(2)}, u32[]{:S(2)}) collective-permute-start(bf16[48,6144]{1,0:T(8,128)(2,1)S(1)} %fusion.59), channel_id=1, source_target_pairs={{0,8},{8,16},{16,24},{24,0},{1,9},{9,17},{17,25},{25,1},{2,10},{10... | collective-permute-start | bytes 1769480 | tf_op jit(solution)/shard_map/ppermute | solution.py:18
Sparse Core Ops, SparseCore 0:
  10.3 53.9 all-gather.7
  89.0 105.1 all-reduce.1
  196.4 51.2 all-gather.5
  249.7 49.9 all-gather.9
  301.8 323.2 all-gather.11
